TPU v7x, 32 devices: a whole 2x2x4 slice. The times are simulated.
32 devices in a mesh: dp: 32 (over z, y, x, core).
Axes of the slice: x: 2, y: 2, z: 4, core: 2. Of those that a mesh axis runs over, the one named last changes fastest.
Arguments:
- tokens: bfloat16 [8192, 960], P('dp'), may hold values from -6 to 6
- out_grad: bfloat16 [8192, 960], P('dp'), may hold values from -6 to 6
- segment_ids: int32 [32, 256], P('dp'), may hold values from 0 to 255, as said below
- positions: int32 [32, 256], P('dp'), may hold values from 0 to 255, as said below
- attn_weight: bfloat16 [960, 2560], P(None, 'dp'), as said below
- gate_weight: bfloat16 [960, 2560], P(None, 'dp'), may hold values from -0.1875 to 0.1875
- up_weight: bfloat16 [960, 2560], P(None, 'dp'), may hold values from -0.1875 to 0.1875
- down_weight: bfloat16 [2560, 960], P('dp'), may hold values from -0.15625 to 0.15625
- norm_gains: bfloat16 [1920], P('dp'), may hold values from 0.25 to 1.75
Outputs:
- block_out: bfloat16 [8192, 960], P('dp')
- tokens_grad: float32 [8192, 960], P('dp')
- attn_weight_grad: float32 [960, 2560], P(None, 'dp')
- gate_weight_grad: float32 [960, 2560], P(None, 'dp')
- up_weight_grad: float32 [960, 2560], P(None, 'dp')
- down_weight_grad: float32 [2560, 960], P('dp')
- norm_gains_grad: float32 [1920], P('dp')
Inputs may be any that keep to these rules, and one draw needn't show every extreme that they name: `segment_ids`: in every sequence the ids start at 0 and rise by one where a new document begins; some sequence has a new document at every token. `positions`: A token's offset from the first token of its document; some sequence is a single document. `attn_weight`: projection weights scaled by their fan-in.
All inputs are finite; a program needn't handle non-finite values.
Results may differ from a plain program's by a relative error of at most 0.01.
The roundings to bfloat16 on the way count: a program that leaves them out, or rounds other values in their place, can miss the bound.
Values may be sent and summed in bfloat16 or wider, within the bound.
A program may use at most 256 MiB of HBM per device.

v0:
```python
import jax
import jax.numpy as jnp
from jax import lax
from jax.sharding import PartitionSpec as P

HEADS = 15
KV_HEADS = 5
HEAD_DIM = 64
GROUP = 3
QD = 960
KD = 320
epsilon = 1e-05
rope_base = 10000.0
masked_score = -1e30


def product(form, left, right):
    return jnp.einsum(form, left, right, preferred_element_type=jnp.float32)


def contract(left, right, left_axis, right_axis):
    return lax.dot_general(
        left, right, (((left_axis,), (right_axis,)), ((), ())), preferred_element_type=jnp.float32
    )


def rotate_half(values):
    half_dim = values.shape[-1] // 2
    return jnp.concatenate([-values[..., half_dim:], values[..., :half_dim]], axis=-1)


def rope_tables(positions):
    half_dim = HEAD_DIM // 2
    inverse = rope_base ** (-2.0 * jnp.arange(half_dim).astype(jnp.float32) / HEAD_DIM)
    angles = positions.astype(jnp.float32)[:, None] * inverse[None, :]
    angles = jnp.concatenate([angles, angles], axis=-1)
    return (jnp.cos(angles)[:, None, :], jnp.sin(angles)[:, None, :])


def norm_rows(values, gain):
    inv_rms = lax.rsqrt(jnp.mean(values * values, axis=-1, keepdims=True) + epsilon)
    normed = values * inv_rms
    return (normed, inv_rms, (normed * gain.astype(jnp.float32)).astype(jnp.bfloat16))


def norm_back(grad_in, normed, inv_rms, gain):
    grad_normed = grad_in * gain.astype(jnp.float32)
    grad_gain = jnp.sum(grad_in * normed, axis=0)
    inner_mean = jnp.mean(grad_normed * normed, axis=-1, keepdims=True)
    return (inv_rms * (grad_normed - normed * inner_mean), grad_gain)


def allowed_pairs(segments):
    row_index = jnp.arange(segments.shape[0])
    same_doc = segments[:, None] == segments[None, :]
    return same_doc & (row_index[:, None] >= row_index[None, :])


def scores_of(queries, key_rows, allowed):
    scores = product("qhgd,shd->hgqs", queries, key_rows) * HEAD_DIM ** (-0.5)
    return jnp.where(allowed[None, None], scores, masked_score)


def attend(queries, key_rows, value_rows, allowed):
    scores = scores_of(queries, key_rows, allowed)
    row_max = jnp.max(scores, axis=-1, keepdims=True)
    weights = jnp.exp(scores - row_max)
    totals = jnp.sum(weights, axis=-1, keepdims=True)
    weights_low = (weights / totals).astype(jnp.bfloat16)
    mixed_heads = product("hgqs,shd->qhgd", weights_low, value_rows).astype(jnp.bfloat16)
    return (mixed_heads, row_max + jnp.log(totals))


def attend_back(queries, key_rows, value_rows, allowed, mixed_heads, log_totals, grad_heads):
    scores = scores_of(queries, key_rows, allowed)
    probs_back = jnp.exp(scores - log_totals)
    grad_values = product("hgqs,qhgd->shd", probs_back.astype(jnp.bfloat16), grad_heads)
    grad_probs = product("qhgd,shd->hgqs", grad_heads, value_rows)
    row_dot = jnp.sum(grad_heads.astype(jnp.float32) * mixed_heads.astype(jnp.float32), axis=-1)
    row_dot = jnp.transpose(row_dot, (1, 2, 0))[..., None]
    grad_scores = (probs_back * (grad_probs - row_dot) * HEAD_DIM ** (-0.5)).astype(jnp.bfloat16)
    grad_queries = product("hgqs,shd->qhgd", grad_scores, key_rows)
    grad_keys = product("hgqs,qhgd->shd", grad_scores, queries)
    return (grad_queries, grad_keys, grad_values)


def layer_forward(
    tokens, segments, positions, attn_weight, gate_weight, up_weight, down_weight, norm_gains
):
    seq_len = tokens.shape[0]
    model_width = tokens.shape[1]
    residual = tokens.astype(jnp.float32)
    normed_one, inv_one, input_one = norm_rows(residual, norm_gains[:model_width])
    projected = contract(input_one, attn_weight[:, : QD + 2 * KD], 1, 0)
    cosine, sine_tab = rope_tables(positions)
    query_part = projected[:, :QD].reshape(seq_len, HEADS, HEAD_DIM)
    key_part = projected[:, QD : QD + KD].reshape(seq_len, KV_HEADS, HEAD_DIM)
    queries = (query_part * cosine + rotate_half(query_part) * sine_tab).astype(jnp.bfloat16)
    queries = queries.reshape(seq_len, KV_HEADS, GROUP, HEAD_DIM)
    key_rows = (key_part * cosine + rotate_half(key_part) * sine_tab).astype(jnp.bfloat16)
    value_rows = projected[:, QD + KD :].reshape(seq_len, KV_HEADS, HEAD_DIM).astype(jnp.bfloat16)
    allowed = allowed_pairs(segments)
    mixed_heads, log_totals = attend(queries, key_rows, value_rows, allowed)
    mixed_flat = mixed_heads.reshape(seq_len, QD)
    middle = residual + contract(mixed_flat, attn_weight[:, QD + 2 * KD :], 1, 1)
    normed_two, inv_two, input_two = norm_rows(middle, norm_gains[model_width:])
    gate_act = contract(input_two, gate_weight, 1, 0)
    up_proj = contract(input_two, up_weight, 1, 0)
    hidden = (jax.nn.silu(gate_act) * up_proj).astype(jnp.bfloat16)
    output = middle + contract(hidden, down_weight, 1, 0)
    kept_state = {
        "normed_one": normed_one,
        "inv_one": inv_one,
        "input_one": input_one,
        "cosine": cosine,
        "sine_tab": sine_tab,
        "queries": queries,
        "key_rows": key_rows,
        "value_rows": value_rows,
        "allowed": allowed,
        "mixed_heads": mixed_heads,
        "log_totals": log_totals,
        "normed_two": normed_two,
        "inv_two": inv_two,
        "input_two": input_two,
        "gate_act": gate_act,
        "up_proj": up_proj,
        "hidden": hidden,
    }
    return (output.astype(jnp.bfloat16), kept_state)


def ffn_backward(out_grad, kept_state, gate_weight, up_weight, down_weight, norm_gains):
    model_width = out_grad.shape[1]
    gate_act = kept_state["gate_act"]
    input_two = kept_state["input_two"]
    grad_hidden = contract(out_grad, down_weight, 1, 1)
    grad_down = contract(kept_state["hidden"], out_grad, 0, 0)
    sig_gate = jax.nn.sigmoid(gate_act)
    grad_gate = (
        grad_hidden * kept_state["up_proj"] * sig_gate * (1.0 + gate_act * (1.0 - sig_gate))
    ).astype(jnp.bfloat16)
    grad_up = (grad_hidden * gate_act * sig_gate).astype(jnp.bfloat16)
    grad_gate_w = contract(input_two, grad_gate, 0, 0)
    grad_up_w = contract(input_two, grad_up, 0, 0)
    grad_input_two = contract(grad_gate, gate_weight, 1, 1) + contract(grad_up, up_weight, 1, 1)
    grad_norm_two, grad_gain_two = norm_back(
        grad_input_two, kept_state["normed_two"], kept_state["inv_two"], norm_gains[model_width:]
    )
    grad_middle = out_grad.astype(jnp.float32) + grad_norm_two
    return (grad_middle, grad_gain_two, (grad_gate_w, grad_up_w, grad_down))


def attn_backward(grad_middle, kept_state, attn_weight, norm_gains):
    seq_len = grad_middle.shape[0]
    model_width = grad_middle.shape[1]
    mixed_heads = kept_state["mixed_heads"]
    grad_mid_low = grad_middle.astype(jnp.bfloat16)
    grad_out_proj = contract(grad_mid_low, mixed_heads.reshape(seq_len, QD), 0, 0)
    grad_heads = contract(grad_mid_low, attn_weight[:, QD + 2 * KD :], 1, 0).astype(jnp.bfloat16)
    grad_heads = grad_heads.reshape(seq_len, KV_HEADS, GROUP, HEAD_DIM)
    grad_queries, grad_keys, grad_values = attend_back(
        kept_state["queries"],
        kept_state["key_rows"],
        kept_state["value_rows"],
        kept_state["allowed"],
        mixed_heads,
        kept_state["log_totals"],
        grad_heads,
    )
    cosine = kept_state["cosine"]
    sine_tab = kept_state["sine_tab"]
    grad_q_part = grad_queries.reshape(seq_len, HEADS, HEAD_DIM)
    grad_q_part = grad_q_part * cosine - rotate_half(grad_q_part) * sine_tab
    grad_k_part = grad_keys * cosine - rotate_half(grad_keys) * sine_tab
    grad_projected = jnp.concatenate(
        [
            grad_q_part.reshape(seq_len, QD),
            grad_k_part.reshape(seq_len, KD),
            grad_values.reshape(seq_len, KD),
        ],
        axis=1,
    ).astype(jnp.bfloat16)
    grad_qkv = contract(kept_state["input_one"], grad_projected, 0, 0)
    grad_input_one = contract(grad_projected, attn_weight[:, : QD + 2 * KD], 1, 1)
    grad_norm_one, grad_gain_one = norm_back(
        grad_input_one, kept_state["normed_one"], kept_state["inv_one"], norm_gains[:model_width]
    )
    grad_tokens = grad_middle + grad_norm_one
    grad_attn = jnp.concatenate([grad_qkv, grad_out_proj], axis=1)
    return (grad_tokens, grad_attn, grad_gain_one)


def device_rows(parts, devices):
    widths = [matrix.shape[dim] // devices for matrix, dim in parts]
    per_device = sum(widths)

    def term_rows(start, count):
        blocks_here = count // per_device
        blocks = []
        for (matrix, dim), width in zip(parts, widths):
            piece = matrix
            if dim == 1:
                piece = piece.T
            blocks.append(piece.reshape(blocks_here, width, piece.shape[1]))
        return jnp.concatenate(blocks, axis=1).reshape(blocks_here * per_device, -1)

    return (term_rows, widths, per_device)


def split_rows(summed, parts, widths):
    results = []
    offset = 0
    for (matrix, dim), width in zip(parts, widths):
        block = summed[offset : offset + width]
        results.append(block.T if dim == 1 else block)
        offset = offset + width
    return results


def on_device(
    tokens,
    out_grad,
    segment_ids,
    positions,
    attn_weight,
    gate_weight,
    up_weight,
    down_weight,
    norm_gains,
):
    devices = lax.axis_size("dp")
    gathered = (
        lax.all_gather(attn_weight, "dp", axis=1, tiled=True),
        lax.all_gather(gate_weight, "dp", axis=1, tiled=True),
        lax.all_gather(up_weight, "dp", axis=1, tiled=True),
        lax.all_gather(down_weight, "dp", axis=0, tiled=True),
        lax.all_gather(norm_gains, "dp", axis=0, tiled=True),
    )
    output, kept_state = layer_forward(
        tokens,
        segment_ids[0],
        positions[0],
        gathered[0],
        gathered[1],
        gathered[2],
        gathered[3],
        gathered[4],
    )
    grad_middle, grad_gain_two, ffn_grads = ffn_backward(
        out_grad, kept_state, gathered[1], gathered[2], gathered[3], gathered[4]
    )
    grad_tokens, grad_attn, grad_gain_one = attn_backward(
        grad_middle, kept_state, gathered[0], gathered[4]
    )
    grad_gains = jnp.concatenate([grad_gain_one, grad_gain_two])
    all_parts = [(grad_attn, 1), (ffn_grads[0], 1), (ffn_grads[1], 1), (ffn_grads[2], 0)]
    all_fn, all_widths, all_rows = device_rows(all_parts, devices)
    all_summed = lax.psum_scatter(
        all_fn(jnp.int32(0), all_rows * lax.axis_size("dp")), "dp", scatter_dimension=0, tiled=True
    )
    shares = tuple(split_rows(all_summed, all_parts, all_widths))
    gain_share = lax.psum_scatter(grad_gains, "dp", scatter_dimension=0, tiled=True)
    return (output, grad_tokens, shares[0], shares[1], shares[2], shares[3], gain_share)


def solution(mesh):
    in_specs = (
        P("dp", None),
        P("dp", None),
        P("dp", None),
        P("dp", None),
        P(None, "dp"),
        P(None, "dp"),
        P(None, "dp"),
        P("dp", None),
        P("dp"),
    )
    out_specs = (
        P("dp", None),
        P("dp", None),
        P(None, "dp"),
        P(None, "dp"),
        P(None, "dp"),
        P("dp", None),
        P("dp"),
    )
    return jax.shard_map(
        on_device, mesh=mesh, in_specs=in_specs, out_specs=out_specs, check_vma=False
    )
```

profile of v0, /device:TPU:1, one launch (start us, length us, event | category | flops | bytes accessed | tf_op | source)
XLA Modules:
  0.0 832.3 jit_solution(10276416389014661938)
XLA Ops:
  7.2 0.7 all-gather.5.cloned.1.call-update
  7.9 0.7 all-gather.9.cloned.1.call-update
  8.7 0.7 all-gather.7.cloned.1.call-update
  9.4 0.5 all-gather.11.cloned.1.call-update
  10.0 0.7 convert_element_type.92
  10.7 0.8 dynamic-update-slice
  11.5 41.5 %all-reduce = bf16[1920]{0:T(1024)(128)(2,1)S(1)} all-reduce(bf16[1920]{0:T(1024)(128)(2,1)S(1)} %dynamic-update-slice), channel_id=1, replica_groups=mesh['dp'=32] {'dp'}, use_global_device_ids=true, to_apply=%add | all-reduce | flops 1920 | bytes 7680
  53.3 1.2 fusion.40
  54.6 0.9 fusion.50
  55.4 23.2 %all-gather.5.cloned.1.call-done = bf16[960,2560]{0,1:T(8,128)(2,1)} async-done(((bf16[960,80]{0,1:T(8,128)(2,1)}), bf16[960,2560]{0,1:T(8,128)(2,1)}) %all-gather.5.cloned.1.call-update) | async-done | bytes 4915216 | tf_op jit(solution)/shard_map/all_gather | solution.py:234
  78.7 3.1 fusion.7
  82.4 0.8 fusion.62
  83.2 0.6 fusion.3
  83.7 0.8 fusion.24
  84.6 0.6 copy-done
  85.1 2.6 multiply_reduce_fusion.3
  87.8 0.2 multiply_convert_fusion.3
  88.0 57.3 %all-gather.9.cloned.1.call-done = bf16[960,2560]{0,1:T(8,128)(2,1)} async-done(((bf16[960,80]{0,1:T(8,128)(2,1)}), bf16[960,2560]{0,1:T(8,128)(2,1)}) %all-gather.9.cloned.1.call-update) | async-done | bytes 4915216 | tf_op jit(solution)/shard_map/all_gather | solution.py:236
  145.3 5.6 fusion.64
  150.9 61.1 %all-gather.7.cloned.1.call-done = bf16[960,2560]{0,1:T(8,128)(2,1)} async-done(((bf16[960,80]{0,1:T(8,128)(2,1)}), bf16[960,2560]{0,1:T(8,128)(2,1)}) %all-gather.7.cloned.1.call-update) | async-done | bytes 4915216 | tf_op jit(solution)/shard_map/all_gather | solution.py:235
  212.0 5.5 fusion.63
  217.6 61.0 %all-gather.11.cloned.1.call-done = bf16[2560,960]{1,0:T(8,128)(2,1)} async-done(((bf16[80,960]{1,0:T(8,128)(2,1)}), bf16[2560,960]{1,0:T(8,128)(2,1)}) %all-gather.11.cloned.1.call-update) | async-done | bytes 4915216 | tf_op jit(solution)/shard_map/all_gather | solution.py:237
  278.6 8.7 %multiply_convert_fusion = (bf16[256,2560]{1,0:T(8,128)(2,1)S(1)}, bf16[256,2560]{1,0:T(8,128)(2,1)S(1)}, bf16[256,2560]{1,0:T(8,128)(2,1)}) fusion(f32[256,2560]{1,0:T(8,128)} %fusion.63, f32[256,2560]{1,0:T(8,128)} %fusion.64, bf16[256,960]{0,1:T(8,128)(2,1)S(1)} %copy-done.3, bf16[2560,960]{1,0:T(8,128)(2,1)} %all-gather.11.cloned.1.call-done), kind=kOutput, calls=%fused_computation.16 | convolution fusion | flops 1268776960 | bytes 14581760 | tf_op jit(solution)/shard_map/dot_general | solution.py:22
  287.2 2.2 fusion.65
  289.4 4.9 multiply_reduce_fusion
  294.4 0.3 multiply_add_fusion
  294.7 2.4 fusion.25
  297.3 0.7 fusion.31
  298.1 1.1 fusion.2
  299.2 0.7 convolution_bitcast_fusion
  299.9 0.5 fusion.66
  300.4 2.6 fusion.51
  303.0 5.5 fusion.68
  308.5 5.4 fusion.67
  314.4 0.6 copy-done.14
  315.1 4.0 fusion.45
  319.1 9.6 %maximum_bitcast_fusion = f32[2560,960]{0,1:T(8,128)} fusion(f32[960,960]{1,0:T(8,128)} %fusion.51, f32[960,1600]{1,0:T(8,128)} %fusion.45), kind=kLoop, calls=%fused_computation.1 | loop fusion | flops 2457600 | bytes 19660800 | tf_op jit(solution)/shard_map/transpose | solution.py:204
  328.6 11.3 %copy.33 = f32[2560,960]{1,0:T(8,128)} copy(f32[2560,960]{0,1:T(8,128)} %maximum_bitcast_fusion) | data formatting | bytes 19660800 | tf_op jit(solution)/shard_map/transpose | solution.py:204
  339.9 6.8 fusion.69
  346.8 28.4 %pad_maximum_fusion = f32[32,320,960]{2,1,0:T(8,128)} fusion(f32[32,80,960]{2,1,0:T(8,128)} %bitcast.106, f32[32,80,960]{2,1,0:T(8,128)} %bitcast.104, f32[32,80,960]{2,1,0:T(8,128)} %bitcast.105, f32[32,80,960]{2,1,0:T(8,128)} %bitcast.107), kind=kLoop, calls=%fused_computation | loop fusion | flops 29491200 | bytes 78643200 | tf_op jit(solution)/shard_map/concatenate | solution.py:206
  375.3 0.9 copy-done.15
  376.2 4.4 fusion.39
  380.7 61.1 %all-reduce.1 = f32[1920]{0:T(1024)S(1)} all-reduce(f32[1920]{0:T(1024)S(1)} %pad_maximum_fusion.5), channel_id=3, replica_groups=mesh['dp'=32] {'dp'}, use_global_device_ids=true, to_apply=%region_10.11.clone | all-reduce | flops 1920 | bytes 15360
  441.8 0.6 dynamic-slice
  442.4 2.4 fusion.38
  444.8 5.9 fusion.23
  450.7 372.7 %reduce-scatter.2.cloned.1.call-done = f32[320,960]{1,0:T(8,128)} async-done(((f32[10240,960]{1,0:T(8,128)}), f32[320,960]{1,0:T(8,128)}) %reduce-scatter.2.cloned.1.call-update) | async-done | bytes 1228816 | tf_op jit(solution)/shard_map/reduce_scatter | solution.py:259
  823.5 2.3 fusion.61
  (65 shorter events, 1.9 us)
Async XLA Ops:
  7.2 71.5 %all-gather.5.cloned.1.call-start = ((), (), s32[]{:S(2)}) async-start(), calls=%async_computation.1 | async-start | bytes 5406720 | tf_op jit(solution)/shard_map/all_gather | solution.py:234
  7.9 137.4 %all-gather.9.cloned.1.call-start = ((), (), s32[]{:S(2)}) async-start(), calls=%async_computation.3 | async-start | bytes 5406720 | tf_op jit(solution)/shard_map/all_gather | solution.py:236
  8.6 203.4 %all-gather.7.cloned.1.call-start = ((), (), s32[]{:S(2)}) async-start(), calls=%async_computation.2 | async-start | bytes 5406720 | tf_op jit(solution)/shard_map/all_gather | solution.py:235
  9.4 269.2 %all-gather.11.cloned.1.call-start = ((), (), s32[]{:S(2)}) async-start(), calls=%async_computation.4 | async-start | bytes 5406720 | tf_op jit(solution)/shard_map/all_gather | solution.py:237
  10.0 813.5 %reduce-scatter.2.cloned.1.call-start = ((), (), s32[]{:S(2)}) async-start(), calls=%async_computation.5 | async-start | bytes 43253760 | tf_op jit(solution)/shard_map/reduce_scatter | solution.py:259
  53.3 28.9 %copy-start.8 = (f32[256,64]{0,1:T(8,128)}, f32[256,64]{0,1:T(8,128)S(1)}, u32[]{:S(2)}) copy-start(f32[256,64]{0,1:T(8,128)S(1)} %get-tuple-element.27) | copy-start | bytes 196612
  81.8 1.9 copy-start.12
  82.0 1.1 copy-start.10
  83.1 2.0 copy-start
  83.7 1.4 copy-start.2
  85.1 2.7 copy-start.6
  150.9 127.7 %copy-start.3 = (bf16[256,960]{0,1:T(8,128)(2,1)S(1)}, bf16[256,960]{0,1:T(8,128)(2,1)}, u32[]{:S(2)}) copy-start(bf16[256,960]{0,1:T(8,128)(2,1)} %param.10) | copy-start | bytes 1474564
  278.6 8.7 %copy-start.18 = (bf16[960,2560]{0,1:T(8,128)(2,1)S(1)}, bf16[960,2560]{0,1:T(8,128)(2,1)}, u32[]{:S(2)}) copy-start(bf16[960,2560]{0,1:T(8,128)(2,1)} %all-gather.7.cloned.1.call-done) | copy-start | bytes 14745604
  289.4 4.9 copy-start.4
  294.3 2.8 copy-start.7
  294.4 2.9 copy-start.1
  294.7 3.4 copy-start.13
  298.0 16.4 %copy-start.16 = (bf16[5,64,256]{2,1,0:T(8,128)(2,1)}, bf16[5,64,256]{2,1,0:T(8,128)(2,1)S(1)}, u32[]{:S(2)}) copy-start(bf16[5,64,256]{2,1,0:T(8,128)(2,1)S(1)} %fusion.31) | copy-start | bytes 491524
  298.1 1.9 copy-start.11
  308.5 5.5 copy-start.9
  314.4 0.7 copy-start.14
  328.6 11.3 %copy-start.5 = (bf16[256,960]{0,1:T(8,128)(2,1)S(1)}, bf16[256,960]{0,1:T(8,128)(2,1)}, u32[]{:S(2)}) copy-start(bf16[256,960]{0,1:T(8,128)(2,1)} %param.10) | copy-start | bytes 1474564
  375.2 0.9 copy-start.15
  375.2 1.0 copy-start.17
Sparse Core Ops, SparseCore 0:
  10.8 67.7 all-gather.4
  81.5 63.7 all-gather.8
  148.2 63.7 all-gather.6
  214.8 63.7 all-gather.10
  375.4 448.0 reduce-scatter.1
where the time goes:
time: 833 us; the launch traced here: 832 us
  waiting for transfers between devices  578 us (69%)
  blocking collectives  103 us (12%)
  matrix products  74.3 us (9%)
  other arithmetic  45.6 us (5%)
  local copies, waits for them, and re-layouts  17.4 us (2%)
  between operations  14.2 us (2%)
    reduce_scatter x1, waiting for transfers between devices, on_device(): lax.psum_scatter(all_fn(jnp.int32(0), all_rows * lax.axis_size('dp')), 'd...  373 us
    unnamed x2, blocking collectives  103 us
    dot_general x15, matrix products, contract(): lax.dot_general(left, right, (((left_axis,), (right_axis,)), ((), ())), p...  69.7 us
    all_gather x1, waiting for transfers between devices, on_device(): lax.all_gather(gate_weight, 'dp', axis=1, tiled=True)  61.1 us
    all_gather x1, waiting for transfers between devices, on_device(): lax.all_gather(down_weight, 'dp', axis=0, tiled=True)  61 us
    all_gather x1, waiting for transfers between devices, on_device(): lax.all_gather(up_weight, 'dp', axis=1, tiled=True)  57.3 us
    concatenate x1, other arithmetic, term_rows(): return jnp.concatenate(blocks, axis=1).reshape(blocks_here * per_device, -1)  28.4 us
    all_gather x1, waiting for transfers between devices, on_device(): lax.all_gather(attn_weight, 'dp', axis=1, tiled=True)  23.2 us
  transfers between devices with their start and end apart: 5, of which 5 were waited for; matrix products, arithmetic and copies ran while one was open for 4% of the time, Pallas kernels for 0%

commit v1 on v0

--- a/solution.py
+++ b/solution.py
@@ -12,6 +12,29 @@
 epsilon = 1e-05
 rope_base = 10000.0
 masked_score = -1e30
+
+
+def laid_out(blocks, dim):
+    blocks = jnp.moveaxis(blocks, 0, dim)
+    shape = blocks.shape
+    return blocks.reshape(*shape[:dim], shape[dim] * shape[dim + 1], *shape[dim + 2 :])
+
+
+def grow_blocks(x, axis):
+    count, place = (lax.axis_size(axis), lax.axis_index(axis))
+    blocks, bit = (x[None], 1)
+    while bit < count:
+        received = lax.ppermute(blocks, axis, [(i, i ^ bit) for i in range(count)])
+        low = place & bit == 0
+        blocks = jnp.concatenate(
+            [jnp.where(low, blocks, received), jnp.where(low, received, blocks)]
+        )
+        bit *= 2
+    return blocks
+
+
+def doubled_up(array, axis, dim):
+    return laid_out(grow_blocks(array, axis), dim)
 
 
 def product(form, left, right):
@@ -233,7 +256,7 @@
     gathered = (
         lax.all_gather(attn_weight, "dp", axis=1, tiled=True),
         lax.all_gather(gate_weight, "dp", axis=1, tiled=True),
-        lax.all_gather(up_weight, "dp", axis=1, tiled=True),
+        doubled_up(up_weight, "dp", 1),
         lax.all_gather(down_weight, "dp", axis=0, tiled=True),
         lax.all_gather(norm_gains, "dp", axis=0, tiled=True),
     )

time: 833 us -> 870 us (1.044)
  blocking collectives: 103 us -> 207 us
  waiting for transfers between devices: 578 us -> 500 us
    unnamed x2, blocking collectives: 103 us -> 207 us
    ppermute x0 -> x5, waiting for transfers between devices: none -> 73.4 us  [grow_blocks(): received = lax.ppermute(blocks, axis, [(i, i ^ bit) for i in range(count)])]
    all_gather x1, waiting for transfers between devices: 61 us -> 0.02 us  [on_device(): lax.all_gather(down_weight, 'dp', axis=0, tiled=True)]
    all_gather x1 -> x0, waiting for transfers between devices: 57.3 us -> none  [on_device(): lax.all_gather(up_weight, 'dp', axis=1, tiled=True)]
    all_gather x1, waiting for transfers between devices: 23.2 us -> 0.01 us  [on_device(): lax.all_gather(attn_weight, 'dp', axis=1, tiled=True)]
    all_gather x1, waiting for transfers between devices: 61.1 us -> 52.2 us  [on_device(): lax.all_gather(gate_weight, 'dp', axis=1, tiled=True)]
  transfers between devices with their start and end apart: 5 -> 9, of which waited for: 5 -> 6; matrix products, arithmetic and copies ran while one was open for 4% -> 4% of each run, Pallas kernels for 0% -> 0%
where the time goes in v1:
time: 870 us; the launch traced here: 869 us
  waiting for transfers between devices  500 us (57%)
  blocking collectives  207 us (24%)
  matrix products  69.9 us (8%)
  other arithmetic  53 us (6%)
  local copies, waits for them, and re-layouts  17.8 us (2%)
  between operations  14.2 us (2%)
    reduce_scatter x1, waiting for transfers between devices, on_device(): lax.psum_scatter(all_fn(jnp.int32(0), all_rows * lax.axis_size('dp')), 'd...  373 us
    unnamed x2, blocking collectives  207 us
    ppermute x5, waiting for transfers between devices, grow_blocks(): received = lax.ppermute(blocks, axis, [(i, i ^ bit) for i in range(count)])  73.4 us
    dot_general x15, matrix products, contract(): lax.dot_general(left, right, (((left_axis,), (right_axis,)), ((), ())), p...  65.2 us
    all_gather x1, waiting for transfers between devices, on_device(): lax.all_gather(gate_weight, 'dp', axis=1, tiled=True)  52.2 us
    concatenate x1, other arithmetic, term_rows(): return jnp.concatenate(blocks, axis=1).reshape(blocks_here * per_device, -1)  28.5 us
  transfers between devices with their start and end apart: 9, of which 6 were waited for; matrix products, arithmetic and copies ran while one was open for 4% of the time, Pallas kernels for 0%

profile of v1, /device:TPU:1, one launch (start us, length us, event | category | flops | bytes accessed | tf_op | source)
XLA Modules:
  0.0 868.8 jit_solution(16141494905438458641)
XLA Ops:
  7.2 0.7 all-gather.4.cloned.1.call-update
  7.9 0.7 all-gather.8.cloned.1.call-update
  8.8 1.6 collective-permute-done
  10.4 0.9 broadcast_select_fusion.9
  11.4 2.4 collective-permute-start.1
  13.8 7.7 collective-permute-done.1
  21.6 1.3 collective-permute-start.2
  23.0 16.1 %collective-permute-done.2 = bf16[4,960,80]{1,2,0:T(8,128)(2,1)S(1)} collective-permute-done((bf16[4,960,80]{1,2,0:T(8,128)(2,1)S(1)}, bf16[4,960,80]{1,2,0:T(8,128)(2,1)S(1)}, u32[]{:S(2)}, u32[]{:S(2)}) %collective-permute-start.2) | collective-permute-done | bytes 614432 | tf_op jit(solution)/shard_map/ppermute | solution.py:27
  39.2 0.8 copy-done.2
  40.1 1.3 collective-permute-start.3
  41.4 48.1 %collective-permute-done.3 = bf16[8,960,80]{1,2,0:T(8,128)(2,1)} collective-permute-done((bf16[8,960,80]{1,2,0:T(8,128)(2,1)S(1)}, bf16[8,960,80]{1,2,0:T(8,128)(2,1)}, u32[]{:S(2)}, u32[]{:S(2)}) %collective-permute-start.3) | collective-permute-done | bytes 1228832 | tf_op jit(solution)/shard_map/ppermute | solution.py:27
  89.4 1.7 broadcast_select_fusion.3
  91.2 1.7 pad_maximum_fusion.2
  92.9 1.3 collective-permute-start.4
  94.5 146.0 %all-reduce = bf16[1920]{0:T(1024)(128)(2,1)S(1)} all-reduce(bf16[1920]{0:T(1024)(128)(2,1)S(1)} %dynamic-update-slice), channel_id=1, replica_groups=mesh['dp'=32] {'dp'}, use_global_device_ids=true, to_apply=%add | all-reduce | flops 1920 | bytes 7680
  241.1 2.2 broadcast_select_fusion.1
  243.3 2.9 pad_maximum_fusion.1
  246.2 3.1 fusion.7
  249.8 0.8 copy-done.4
  250.6 0.8 fusion.62
  251.9 0.8 fusion.24
  252.7 0.6 copy-done
  253.3 2.7 multiply_reduce_fusion.3
  256.3 5.6 fusion.64
  261.9 52.2 %all-gather.6.cloned.1.call-done = bf16[960,2560]{0,1:T(8,128)(2,1)} async-done(((bf16[960,80]{0,1:T(8,128)(2,1)}), bf16[960,2560]{0,1:T(8,128)(2,1)}) %all-gather.6.cloned.1.call-update) | async-done | bytes 4915216 | tf_op jit(solution)/shard_map/all_gather | solution.py:258
  314.2 4.2 fusion.63
  318.4 8.3 multiply_convert_fusion
  326.7 2.2 fusion.65
  329.0 2.4 multiply_reduce_fusion
  331.7 2.4 fusion.25
  334.4 0.7 fusion.31
  335.2 1.1 fusion.2
  336.3 0.7 convolution_bitcast_fusion
  337.5 2.6 fusion.51
  340.1 5.6 fusion.68
  345.7 5.4 fusion.67
  351.5 4.0 fusion.45
  355.5 9.6 %maximum_bitcast_fusion = f32[2560,960]{0,1:T(8,128)} fusion(f32[960,960]{1,0:T(8,128)} %fusion.51, f32[960,1600]{1,0:T(8,128)} %fusion.45), kind=kLoop, calls=%fused_computation.1 | loop fusion | flops 2457600 | bytes 19660800 | tf_op jit(solution)/shard_map/transpose | solution.py:227
  365.1 11.2 %copy.33 = f32[2560,960]{1,0:T(8,128)} copy(f32[2560,960]{0,1:T(8,128)} %maximum_bitcast_fusion) | data formatting | bytes 19660800 | tf_op jit(solution)/shard_map/transpose | solution.py:227
  376.3 6.9 fusion.69
  383.2 28.5 %pad_maximum_fusion = f32[32,320,960]{2,1,0:T(8,128)} fusion(f32[32,80,960]{2,1,0:T(8,128)} %bitcast.112, f32[32,80,960]{2,1,0:T(8,128)} %bitcast.110, f32[32,80,960]{2,1,0:T(8,128)} %bitcast.111, f32[32,80,960]{2,1,0:T(8,128)} %bitcast.113), kind=kLoop, calls=%fused_computation | loop fusion | flops 29491200 | bytes 78643200 | tf_op jit(solution)/shard_map/concatenate | solution.py:229
  411.7 0.9 copy-done.12
  412.6 4.4 fusion.39
  417.1 61.3 %all-reduce.1 = f32[1920]{0:T(1024)S(1)} all-reduce(f32[1920]{0:T(1024)S(1)} %pad_maximum_fusion.10), channel_id=3, replica_groups=mesh['dp'=32] {'dp'}, use_global_device_ids=true, to_apply=%region_10.11.clone | all-reduce | flops 1920 | bytes 15360
  478.9 2.4 fusion.38
  481.4 5.5 fusion.23
  486.8 373.1 %reduce-scatter.2.cloned.1.call-done = f32[320,960]{1,0:T(8,128)} async-done(((f32[10240,960]{1,0:T(8,128)}), f32[320,960]{1,0:T(8,128)}) %reduce-scatter.2.cloned.1.call-update) | async-done | bytes 1228816 | tf_op jit(solution)/shard_map/reduce_scatter | solution.py:282
  859.9 2.3 fusion.61
  (86 shorter events, 5.1 us)
Async XLA Ops:
  7.2 239.0 %all-gather.4.cloned.1.call-start = ((), (), s32[]{:S(2)}) async-start(), calls=%async_computation.1 | async-start | bytes 5406720 | tf_op jit(solution)/shard_map/all_gather | solution.py:257
  7.9 248.4 %all-gather.8.cloned.1.call-start = ((), (), s32[]{:S(2)}) async-start(), calls=%async_computation.3 | async-start | bytes 5406720 | tf_op jit(solution)/shard_map/all_gather | solution.py:260
  8.7 305.5 %all-gather.6.cloned.1.call-start = ((), (), s32[]{:S(2)}) async-start(), calls=%async_computation.2 | async-start | bytes 5406720 | tf_op jit(solution)/shard_map/all_gather | solution.py:258
  8.7 1.7 collective-permute-start
  11.4 10.1 %collective-permute-start.1 = (bf16[2,960,80]{1,2,0:T(8,128)(2,1)S(1)}, bf16[2,960,80]{1,2,0:T(8,128)(2,1)S(1)}, u32[]{:S(2)}, u32[]{:S(2)}) collective-permute-start(bf16[2,960,80]{1,2,0:T(8,128)(2,1)S(1)} %pad_maximum_fusion.8), channel_id=1, source_target_pairs={{0,2},{1,3},{2,0},{3,1},{4,6},{5,7},{6,4},{7,5},{8,10},{9,11},{10,... | collective-permute-start | bytes 921608 | tf_op jit(solution)/shard_map/ppermute | solution.py:27
  21.6 17.4 %collective-permute-start.2 = (bf16[4,960,80]{1,2,0:T(8,128)(2,1)S(1)}, bf16[4,960,80]{1,2,0:T(8,128)(2,1)S(1)}, u32[]{:S(2)}, u32[]{:S(2)}) collective-permute-start(bf16[4,960,80]{1,2,0:T(8,128)(2,1)S(1)} %pad_maximum_fusion.5), channel_id=1, source_target_pairs={{0,4},{1,5},{2,6},{3,7},{4,0},{5,1},{6,2},{7,3},{8,12},{9,13},{10,... | collective-permute-start | bytes 1843208 | tf_op jit(solution)/shard_map/ppermute | solution.py:27
  22.9 837.0 %reduce-scatter.2.cloned.1.call-start = ((), (), s32[]{:S(2)}) async-start(), calls=%async_computation.4 | async-start | bytes 43253760 | tf_op jit(solution)/shard_map/reduce_scatter | solution.py:282
  39.2 0.8 copy-start.2
  40.1 49.3 %collective-permute-start.3 = (bf16[8,960,80]{1,2,0:T(8,128)(2,1)S(1)}, bf16[8,960,80]{1,2,0:T(8,128)(2,1)}, u32[]{:S(2)}, u32[]{:S(2)}) collective-permute-start(bf16[8,960,80]{1,2,0:T(8,128)(2,1)S(1)} %pad_maximum_fusion.3), channel_id=1, source_target_pairs={{0,8},{1,9},{2,10},{3,11},{4,12},{5,13},{6,14},{7,15},{8,0},{9,1},... | collective-permute-start | bytes 3686408 | tf_op jit(solution)/shard_map/ppermute | solution.py:27
  91.1 3.1 copy-start.14
  91.1 3.1 copy-start.15
  91.1 149.6 %copy-start.3 = (bf16[256,960]{0,1:T(8,128)(2,1)S(1)}, bf16[256,960]{0,1:T(8,128)(2,1)}, u32[]{:S(2)}) copy-start(bf16[256,960]{0,1:T(8,128)(2,1)} %param.9) | copy-start | bytes 1474564
  91.2 149.8 %copy-start.13 = (s32[1,256]{1,0:T(1,128)S(1)}, s32[1,256]{1,0:T(1,128)}, u32[]{:S(2)}) copy-start(s32[1,256]{1,0:T(1,128)} %param.11) | copy-start | bytes 3076
  92.9 148.2 %collective-permute-start.4 = (bf16[16,960,80]{1,2,0:T(8,128)(2,1)}, bf16[16,960,80]{1,2,0:T(8,128)(2,1)}, u32[]{:S(2)}, u32[]{:S(2)}) collective-permute-start(bf16[16,960,80]{1,2,0:T(8,128)(2,1)} %pad_maximum_fusion.2), channel_id=1, source_target_pairs={{0,16},{1,17},{2,18},{3,19},{4,20},{5,21},{6,22},{7,23},{8,24},{9,... | collective-permute-start | bytes 7372808 | tf_op jit(solution)/shard_map/ppermute | solution.py:27
  249.8 0.8 copy-start.4
  251.3 2.0 copy-start
  253.3 2.9 copy-start.8
  253.3 3.0 copy-start.6
  314.2 12.6 %slice-start.2 = ((s8[5242880]{0:T(1024)(128)(4,1)}), s8[4194304]{0:T(1024)(128)(4,1)S(1)}, s32[]{:S(2)}) async-start(s8[5242880]{0:T(1024)(128)(4,1)} %bitcast.140), calls=%async_computation.7 | async-start | bytes 8388608
  314.2 14.8 %slice-start = ((s8[5242880]{0:T(1024)(128)(4,1)}), s8[4194304]{0:T(1024)(128)(4,1)S(1)}, s32[]{:S(2)}) async-start(s8[5242880]{0:T(1024)(128)(4,1)} %bitcast.115), calls=%async_computation.5 | async-start | bytes 8388608
  318.4 8.4 slice-start.3
  318.4 10.5 %slice-start.1 = ((s8[5242880]{0:T(1024)(128)(4,1)}), s8[1048576]{0:T(1024)(128)(4,1)S(1)}, s32[]{:S(2)}) async-start(s8[5242880]{0:T(1024)(128)(4,1)} %bitcast.115), calls=%async_computation.6 | async-start | bytes 2097152
  329.0 2.4 copy-start.7
  331.3 2.7 copy-start.9
  331.7 2.7 copy-start.1
  335.2 16.4 %copy-start.11 = (bf16[5,64,256]{2,1,0:T(8,128)(2,1)}, bf16[5,64,256]{2,1,0:T(8,128)(2,1)S(1)}, u32[]{:S(2)}) copy-start(bf16[5,64,256]{2,1,0:T(8,128)(2,1)S(1)} %fusion.31) | copy-start | bytes 491524
  335.2 1.2 copy-start.5
  411.7 0.9 copy-start.12
  478.3 3.0 copy-start.10
Sparse Core Ops, SparseCore 0:
  10.8 77.3 all-gather.3
  91.1 155.9 all-gather.7
  250.0 64.1 all-gather.5
  411.8 448.0 reduce-scatter.1
